TPU v7x, 128 devices: a whole 4x4x4 slice. The times are simulated.
128 devices in a mesh: angle: 16 (over y, x), block: 8 (over z, core).
Axes of the slice: x: 4, y: 4, z: 4, core: 2. Of those that a mesh axis runs over, the one named last changes fastest.
Arguments:
- object_field: float32 [32, 2, 512, 512], P(None, None, 'block'), may hold values from -1.5 to 1.5
- shears: int32 [16, 32], P('angle'), may hold values from -16 to 16, as said below
- positions: int32 [16, 8, 2], P('angle', 'block'), may hold values from 0 to 511
- measured: bfloat16 [16, 8, 512, 512], P('angle', 'block'), may hold values from 0 to 2
- probe_field: float32 [2, 512, 512], replicated
- kappa_field: float32 [16, 512, 512], P('angle'), may hold values from 0.01 to 0.1
Outputs:
- updated_object: float32 [32, 2, 512, 512], P(None, None, 'block')
Inputs may be any that keep to these rules, and one draw needn't show every extreme that they name: `shears`: each angle's row offset of each slice; the values -16 and 16 occur in every draw.
All inputs are finite; a program needn't handle non-finite values.
Results may differ from a plain program's by a relative error of at most 0.0003.
Values sent between devices are 32-bit elements; how exact they have to be, the bound alone decides.
No kernel may reach another device: no remote copies, remote signals or barrier semaphores. Data moves between devices by JAX's collectives and lax.ppermute only.
A program may use at most 192 MiB of HBM per device.

v0:
```python
import jax
import jax.numpy as jnp
from jax import lax
from jax.sharding import PartitionSpec as P

NX = 512
NY = 512
STEPS = 2
SH = 16


def with_halo(x, sides, width):
    for axis, dim in sides:
        count, length = (lax.axis_size(axis), x.shape[dim])
        up = [(i, (i + 1) % count) for i in range(count)]
        down = [(j, i) for i, j in up]
        last = lax.slice_in_dim(x, length - width, length, axis=dim)
        first = lax.slice_in_dim(x, 0, width, axis=dim)
        before = lax.ppermute(last, axis, up)
        after = lax.ppermute(first, axis, down)
        x = jnp.concatenate([before, x, after], axis=dim)
    return x


def laplace(field):
    return (
        jnp.roll(field, 1, -2)
        + jnp.roll(field, -1, -2)
        + jnp.roll(field, 1, -1)
        + jnp.roll(field, -1, -1)
        - 4.0 * field
    )


def frame_loss(projected, probe_field, kappa_row, offset, observed):
    window = jnp.roll(projected, (-offset[0], -offset[1]), axis=(1, 2))
    real_part = probe_field[0] * window[0] - probe_field[1] * window[1]
    imag_part = probe_field[0] * window[1] + probe_field[1] * window[0]
    for step in range(STEPS):
        real_part, imag_part = (
            real_part - kappa_row * laplace(imag_part),
            imag_part + kappa_row * laplace(real_part),
        )
    misfit = real_part * real_part + imag_part * imag_part - observed.astype(jnp.float32)
    return 0.5 * jnp.sum(misfit * misfit)


def per_device(object_field, shears, positions, measured, probe_field, kappa_field):
    strip_rows = object_field.shape[2]
    shear_row = shears[0]
    extended = with_halo(object_field, (("block", 2),), SH)

    def slice_rows(slab, amount):
        return lax.dynamic_slice_in_dim(slab, SH + amount, strip_rows, 1)

    own_strip = jnp.sum(jax.vmap(slice_rows)(extended, shear_row), axis=0)
    projected = lax.all_gather(own_strip, "block", axis=1, tiled=True)
    intensity = probe_field[0] * probe_field[0] + probe_field[1] * probe_field[1]
    kappa_row = kappa_field[0]

    def per_frame(totals, frame_in):
        offset, observed = frame_in
        grads = jax.grad(frame_loss)(projected, probe_field, kappa_row, offset, observed)
        weight = jnp.roll(intensity, (offset[0], offset[1]), axis=(0, 1))
        return (totals + jnp.concatenate([grads, weight[None]], 0), None)

    totals, _ = lax.scan(
        per_frame, jnp.zeros((3, NX, NY), jnp.float32), (positions[0], measured[0])
    )
    strip_totals = lax.psum_scatter(totals, "block", scatter_dimension=1, tiled=True)
    gradient_rim = with_halo(strip_totals, (("block", 1),), SH)

    def unshear_rows(rim_block, amount):
        return lax.dynamic_slice_in_dim(rim_block, SH - amount, strip_rows, 1)

    unsheared = jax.vmap(lambda amount: unshear_rows(gradient_rim, amount))(shear_row)
    summed = lax.psum(unsheared, "angle")
    return object_field - summed[:, :2] / (summed[:, 2:3] + 1.0)


def solution(mesh):
    placed = (
        P(None, None, "block", None),
        P("angle", None),
        P("angle", "block", None),
        P("angle", "block", None, None),
        P(),
        P("angle", None, None),
    )
    return jax.shard_map(
        per_device,
        mesh=mesh,
        in_specs=placed,
        out_specs=P(None, None, "block", None),
        check_vma=False,
    )
```

profile of v0, /device:TPU:1, one launch (start us, length us, event | category | flops | bytes accessed | tf_op | source)
XLA Modules:
  0.0 588.4 jit_solution(2454463777330651448)
XLA Ops:
  6.5 14.3 %copy.27 = f32[32,2,64,512]{3,1,0,2:T(2,128)S(1)} copy(f32[32,2,64,512]{3,2,1,0:T(8,128)} %param.6) | data formatting | bytes 16777216 | tf_op args[0]
  20.9 2.3 fusion.41
  23.2 3.0 collective-permute-start
  26.2 23.0 %collective-permute-done = f32[32,2,16,512]{3,1,0,2:T(2,128)S(1)} collective-permute-done((f32[32,2,16,512]{3,1,0,2:T(2,128)S(1)}, f32[32,2,16,512]{3,1,0,2:T(2,128)S(1)}, u32[]{:S(2)}, u32[]{:S(2)}) %collective-permute-start) | collective-permute-done | bytes 2097184 | tf_op jit(solution)/shard_map/ppermute | solution.py:19
  49.2 2.5 collective-permute-done.1
  51.7 26.0 %pad_maximum_fusion = f32[32,2,96,512]{3,1,0,2:T(2,128)} fusion(f32[32,2,16,512]{3,1,0,2:T(2,128)S(1)} %collective-permute-done.1, f32[32,2,64,512]{3,1,0,2:T(2,128)S(1)} %copy.27, f32[32,2,16,512]{3,1,0,2:T(2,128)S(1)} %collective-permute-done), kind=kLoop, calls=%fused_computation.2 | loop fusion | flops 6291456 | bytes 25165824 | tf_op jit(solution)/shard_map/concatenate | solution.py:21
  77.7 16.2 %gather_fusion.1 = f32[32,2,64,512]{3,1,2,0:T(2,128)} fusion(f32[32,2,96,512]{3,1,0,2:T(2,128)} %pad_maximum_fusion, s32[32]{0:T(128)S(1)} %get-tuple-element.115), kind=kCustom, calls=%fused_computation.1 | custom fusion | bytes 16777728 | tf_op jit(solution)/shard_map/vmap()/gather | solution.py:54
  94.0 6.8 %reduce_sum.9 = f32[2,64,512]{2,0,1:T(2,128)} reduce(f32[32,2,64,512]{3,1,2,0:T(2,128)} %gather_fusion.1, f32[]{:T(128)} %constant.99.clone.1), dimensions={0}, to_apply=%region_0.0 | reduce | flops 2031616 | bytes 8650756 | tf_op jit(solution)/shard_map/reduce_sum | solution.py:56
  106.7 21.5 %all-gather.2.cloned.1.call-done = f32[2,512,512]{2,0,1:T(2,128)} async-done(((f32[2,64,512]{2,0,1:T(2,128)}), f32[2,512,512]{2,0,1:T(2,128)}) %all-gather.2.cloned.1.call-update) | async-done | bytes 2097168 | tf_op jit(solution)/shard_map/all_gather | solution.py:57
  128.2 5.8 fusion.3
  133.9 4.5 fusion.2
  141.8 12.8 %fusion.16 = (f32[512,512]{1,0:T(8,128)S(1)}, f32[512,512]{1,0:T(8,128)S(1)}) fusion(f32[511,512]{1,0:T(8,128)S(1)} %get-tuple-element.111, f32[1,512]{1,0:T(1,128)S(1)} %get-tuple-element.113, f32[1,512]{1,0:T(1,128)S(1)} %get-tuple-element.112, f32[511,512]{1,0:T(8,128)S(1)} %get-tuple-element.110, f32[512,511]{1,0:T(8,128)S(1)} %get-tuple-element.107, ...), kind=kLoop, calls=%fused_computation.35 | loop fusion | flops 3670016 | bytes 12582912 | tf_op jit(solution)/shard_map/while/body/eval_jaxpr/jvp()/sub | solution.py:41
  157.9 2.3 bitcast_multiply_fusion.5
  164.1 2.4 fusion.34
  171.1 3.1 broadcast_in_dim.37
  174.2 96.8 %dynamic_update_slice.10 = f32[2,512,1024]{2,0,1:T(2,128)} dynamic-update-slice(f32[2,512,1024]{2,0,1:T(2,128)} %broadcast_in_dim.37, f32[2,512,512]{2,0,1:T(2,128)S(1)} %copy.31, s32[]{:T(128)} %constant.100.clone.1, s32[]{:T(128)} %constant.100.clone.1, s32[]{:T(128)S(6)} %select_n.79) | dynamic-update-slice | bytes 4194308 | tf_op jit(solution)/shard_map/while/body/eval_jaxpr/transpose(jvp(jit(_roll_dynamic)))/dynamic_update_slice | solution.py:36
  277.4 3.9 pad_maximum_fusion.1
  282.6 70.1 %all-reduce.42.cloned.1.call-done = f32[3,512,512]{2,0,1:T(4,128)} async-done(((f32[3,512,512]{2,0,1:T(4,128)}), f32[3,512,512]{2,0,1:T(4,128)}) %all-reduce.42.cloned.1.call-update) | async-done | bytes 3145744
  357.3 1.7 collective-permute-done.3
  359.1 12.3 %gather_fusion = f32[32,3,64,512]{3,1,2,0:T(4,128)} fusion(f32[3,96,512]{2,0,1:T(4,128)S(1)} %pad_maximum_fusion.2, s32[32]{0:T(128)S(1)} %get-tuple-element.114), kind=kCustom, calls=%fused_computation | custom fusion | bytes 25166208 | tf_op jit(solution)/shard_map/vmap()/gather | solution.py:74
  371.4 15.5 %copy.32 = f32[32,3,64,512]{3,2,1,0:T(8,128)} copy(f32[32,3,64,512]{3,1,2,0:T(4,128)} %gather_fusion) | data formatting | bytes 25165824 | tf_op jit(solution)/shard_map/vmap()/gather | solution.py:74
  387.0 182.0 %all-reduce.40.cloned.1.call-done = f32[32,3,64,512]{3,2,1,0:T(8,128)} async-done(((f32[32,3,64,512]{3,2,1,0:T(8,128)}), f32[32,3,64,512]{3,2,1,0:T(8,128)}) %all-reduce.40.cloned.1.call-update) | async-done | bytes 12582928 | tf_op jit(solution)/shard_map/psum | solution.py:77
  569.0 2.9 fusion.1
  571.9 9.6 %fusion = f32[32,2,64,512]{3,2,1,0:T(8,128)} fusion(f32[32,2,64,512]{3,2,1,0:T(8,128)} %param.6, f32[32,3,64,512]{3,2,1,0:T(8,128)} %all-reduce.40.cloned.1.call-done, f32[32,64,512]{2,1,0:T(8,128)S(1)} %fusion.1), kind=kLoop, calls=%fused_computation.4 | loop fusion | flops 4194304 | bytes 29360128 | tf_op jit(solution)/shard_map/sub | solution.py:78
  (74 shorter events, 27.6 us)
Async XLA Ops:
  6.5 121.6 %all-gather.2.cloned.1.call-start = ((), (), s32[]{:S(2)}) async-start(), calls=%async_computation | async-start | bytes 2359296 | tf_op jit(solution)/shard_map/all_gather | solution.py:57
  20.9 5.4 copy-start.5
  23.2 26.0 %collective-permute-start = (f32[32,2,16,512]{3,1,0,2:T(2,128)S(1)}, f32[32,2,16,512]{3,1,0,2:T(2,128)S(1)}, u32[]{:S(2)}, u32[]{:S(2)}) collective-permute-start(f32[32,2,16,512]{3,1,0,2:T(2,128)S(1)} %get-tuple-element.41), channel_id=1, source_target_pairs={{0,1},{1,2},{2,3},{3,4},{4,5},{5,6},{6,7},{7,0},{8,9},{9,10},{10,1... | collective-permute-start | bytes 6291464 | tf_op jit(solution)/shard_map/ppermute | solution.py:19
  26.2 25.5 %collective-permute-start.1 = (f32[32,2,16,512]{3,1,0,2:T(2,128)S(1)}, f32[32,2,16,512]{3,1,0,2:T(2,128)S(1)}, u32[]{:S(2)}, u32[]{:S(2)}) collective-permute-start(f32[32,2,16,512]{3,1,0,2:T(2,128)S(1)} %get-tuple-element.42), channel_id=1, source_target_pairs={{1,0},{2,1},{3,2},{4,3},{5,4},{6,5},{7,6},{0,7},{9,8},{10,9},{11,1... | collective-permute-start | bytes 6291464 | tf_op jit(solution)/shard_map/ppermute | solution.py:20
  94.0 7.2 %copy-start.4 = (s32[1,1,2]{2,1,0:T(1,128)S(1)}, s32[1,1,2]{2,1,0:T(1,128)}, u32[]{:S(2)}) copy-start(s32[1,1,2]{2,1,0:T(1,128)} %param.8) | copy-start | bytes 28
  100.8 251.8 %all-reduce.42.cloned.1.call-start = ((), (), s32[]{:S(2)}) async-start(), calls=%async_computation.2 | async-start | bytes 8388608
  133.9 6.1 %copy-start.1 = (f32[2,512,512]{2,1,0:T(8,128)S(1)}, f32[2,512,512]{2,1,0:T(8,128)}, u32[]{:S(2)}) copy-start(f32[2,512,512]{2,1,0:T(8,128)} %param.10) | copy-start | bytes 6291460
  140.5 1.2 copy-start
  156.9 1.0 copy-start.3
  271.1 2.2 copy-start.2
  277.4 4.0 copy-start.6
  281.4 287.6 %all-reduce.40.cloned.1.call-start = ((), (), s32[]{:S(2)}) async-start(), calls=%async_computation.1 | async-start | bytes 25165824 | tf_op jit(solution)/shard_map/psum | solution.py:77
  353.7 3.6 collective-permute-start.2
  354.5 4.4 collective-permute-start.3
Sparse Core Ops, SparseCore 0:
  100.9 27.1 all-gather.1
  281.5 71.1 all-reduce.41
  387.1 181.8 all-reduce.39
where the time goes:
time: 600 us; the launch traced here: 588 us
  waiting for transfers between devices  301 us (50%)
  local copies, waits for them, and re-layouts  177 us (30%)
  other arithmetic  85.7 us (14%)
  between operations  19.5 us (3%)
    psum x1, waiting for transfers between devices, per_device(): summed = lax.psum(unsheared, 'angle')  182 us
    dynamic_update_slice x1, local copies, waits for them, and re-layouts, frame_loss(): window = jnp.roll(projected, (-offset[0], -offset[1]), axis=(1, 2))  96.8 us
    unnamed x4, waiting for transfers between devices  70.1 us
    gather x2, local copies, waits for them, and re-layouts, unshear_rows(): return lax.dynamic_slice_in_dim(rim_block, SH - amount, strip_rows, 1)  27.8 us
    concatenate x2, other arithmetic, with_halo(): x = jnp.concatenate([before, x, after], axis=dim)  26.2 us
    ppermute x2, waiting for transfers between devices, with_halo(): before = lax.ppermute(last, axis, up)  23 us
    all_gather x1, waiting for transfers between devices, per_device(): projected = lax.all_gather(own_strip, 'block', axis=1, tiled=True)  21.5 us
    unnamed x17, local copies, waits for them, and re-layouts  17.8 us
  transfers between devices with their start and end apart: 7, of which 6 were waited for; matrix products, arithmetic and copies ran while one was open for 0% of the time, Pallas kernels for 0%

commit v1 on v0

--- a/solution.py
+++ b/solution.py
@@ -1,3 +1,4 @@
+import functools
 import jax
 import jax.numpy as jnp
 from jax import lax
@@ -7,6 +8,37 @@
 NY = 512
 STEPS = 2
 SH = 16
+
+
+def spread_spots(work_x, dim_no):
+    arr_now = list(work_x.shape[1:])
+    arr_now[dim_no] *= work_x.shape[0]
+    return jnp.moveaxis(work_x, 0, dim_no).reshape(arr_now)
+
+
+def _track_arrays(vector, bus_axis, pos_dim):
+    world_n = lax.axis_size(bus_axis)
+    copies = [(tick, (tick + 1) % world_n) for tick in range(world_n)]
+    part_next, item_now = ([], [])
+    pool = [(dev_j, jj) for jj, dev_j in copies]
+    for ix in range(world_n - 1):
+        if ix % 2 == 0:
+            part_next.append(
+                lax.ppermute(
+                    part_next[-1] if part_next else vector, perm=copies, axis_name=bus_axis
+                )
+            )
+        else:
+            tmp = lax.ppermute(item_now[-1] if item_now else vector, perm=pool, axis_name=bus_axis)
+            item_now.append(tmp)
+    outcome_arr = jnp.stack([*part_next[::-1], vector, *item_now], 0)
+    local_now = lax.axis_index(bus_axis)
+    now = local_now - len(part_next)
+    outcome_arr = outcome_arr[(jnp.arange(world_n) - now) % world_n]
+    return spread_spots(outcome_arr, pos_dim)
+
+
+series_pass = functools.partial(_track_arrays, bus_axis="block", pos_dim=1)
 
 
 def with_halo(x, sides, width):
@@ -54,7 +86,7 @@
         return lax.dynamic_slice_in_dim(slab, SH + amount, strip_rows, 1)
 
     own_strip = jnp.sum(jax.vmap(slice_rows)(extended, shear_row), axis=0)
-    projected = lax.all_gather(own_strip, "block", axis=1, tiled=True)
+    projected = series_pass(own_strip)
     intensity = probe_field[0] * probe_field[0] + probe_field[1] * probe_field[1]
     kappa_row = kappa_field[0]
 

time: 600 us -> 587 us (0.978)
  other arithmetic: 85.7 us -> 65.4 us
  starting transfers between devices: 5.85 us -> 20.3 us
  waiting for transfers between devices: 301 us -> 287 us
  local copies, waits for them, and re-layouts: 177 us -> 185 us
    all_gather x1 -> x0, waiting for transfers between devices: 21.5 us -> none  [per_device(): projected = lax.all_gather(own_strip, 'block', axis=1, tiled=True)]
    ppermute x0 -> x7, starting transfers between devices: none -> 14.8 us  [the longest x3 7.7 us: _track_arrays(): lax.ppermute(item_now[-1] if item_now else vector, perm=pool, axis_name=b...]
    sub x1, other arithmetic: 12.8 us -> 1.37 us  [frame_loss(): real_part - kappa_row * laplace(imag_part)]
    concatenate x2, other arithmetic: 10.2 us -> 1.85 us  [frame_loss(): window = jnp.roll(projected, (-offset[0], -offset[1]), axis=(1, 2))]
    unnamed x17 -> x24, local copies, waits for them, and re-layouts: 17.8 us -> 24.6 us
    ppermute x0 -> x7, waiting for transfers between devices: none -> 6.5 us  [the longest x4 6.2 us: _track_arrays(): lax.ppermute(part_next[-1] if part_next else vector, perm=copies, axis_na...]
    unnamed x4 -> x3, waiting for transfers between devices: 70.1 us -> 71.9 us
  transfers between devices with their start and end apart: 7 -> 13, of which waited for: 6 -> 10; matrix products, arithmetic and copies ran while one was open for 0% -> 1% of each run, Pallas kernels for 0% -> 0%
where the time goes in v1:
time: 587 us; the launch traced here: 577 us
  waiting for transfers between devices  287 us (49%)
  local copies, waits for them, and re-layouts  185 us (32%)
  other arithmetic  65.4 us (11%)
  starting transfers between devices  20.3 us (3%)
  between operations  19.6 us (3%)
    psum x1, waiting for transfers between devices, per_device(): summed = lax.psum(unsheared, 'angle')  182 us
    dynamic_update_slice x1, local copies, waits for them, and re-layouts, frame_loss(): window = jnp.roll(projected, (-offset[0], -offset[1]), axis=(1, 2))  97 us
    unnamed x3, waiting for transfers between devices  71.9 us
    gather x2, local copies, waits for them, and re-layouts, unshear_rows(): return lax.dynamic_slice_in_dim(rim_block, SH - amount, strip_rows, 1)  27.8 us
    concatenate x2, other arithmetic, with_halo(): x = jnp.concatenate([before, x, after], axis=dim)  26.1 us
    unnamed x24, local copies, waits for them, and re-layouts  24.6 us
    ppermute x2, waiting for transfers between devices, with_halo(): before = lax.ppermute(last, axis, up)  23.6 us
    gather x1, local copies, waits for them, and re-layouts, slice_rows(): return lax.dynamic_slice_in_dim(slab, SH + amount, strip_rows, 1)  16.4 us
  transfers between devices with their start and end apart: 13, of which 10 were waited for; matrix products, arithmetic and copies ran while one was open for 1% of the time, Pallas kernels for 0%

profile of v1, /device:TPU:1, one launch (start us, length us, event | category | flops | bytes accessed | tf_op | source)
XLA Modules:
  0.0 577.3 jit_solution(3759624508228548784)
XLA Ops:
  6.5 14.3 %copy.36 = f32[32,2,64,512]{3,1,0,2:T(2,128)S(1)} copy(f32[32,2,64,512]{3,2,1,0:T(8,128)} %param.6) | data formatting | bytes 16777216 | tf_op args[0]
  23.2 3.0 collective-permute-start
  26.2 23.0 %collective-permute-done = f32[32,2,16,512]{3,1,0,2:T(2,128)S(1)} collective-permute-done((f32[32,2,16,512]{3,1,0,2:T(2,128)S(1)}, f32[32,2,16,512]{3,1,0,2:T(2,128)S(1)}, u32[]{:S(2)}, u32[]{:S(2)}) %collective-permute-start) | collective-permute-done | bytes 2097184 | tf_op jit(solution)/shard_map/ppermute | solution.py:51
  49.2 2.5 collective-permute-done.1
  51.7 26.0 %pad_maximum_fusion = f32[32,2,96,512]{3,1,0,2:T(2,128)} fusion(f32[32,2,16,512]{3,1,0,2:T(2,128)S(1)} %collective-permute-done.1, f32[32,2,64,512]{3,1,0,2:T(2,128)S(1)} %copy.36, f32[32,2,16,512]{3,1,0,2:T(2,128)S(1)} %collective-permute-done), kind=kLoop, calls=%fused_computation.3 | loop fusion | flops 6291456 | bytes 25165824 | tf_op jit(solution)/shard_map/concatenate | solution.py:53
  77.6 16.4 %gather_fusion.2 = f32[32,2,64,512]{3,1,2,0:T(2,128)} fusion(f32[32,2,96,512]{3,1,0,2:T(2,128)} %pad_maximum_fusion, s32[32]{0:T(128)S(1)} %get-tuple-element.113), kind=kCustom, calls=%fused_computation.2 | custom fusion | bytes 16777728 | tf_op jit(solution)/shard_map/vmap()/gather | solution.py:86
  94.1 6.1 %reduce_sum.9 = f32[2,64,512]{2,0,1:T(2,128)S(1)} reduce(f32[32,2,64,512]{3,1,2,0:T(2,128)} %gather_fusion.2, f32[]{:T(128)} %constant.118.clone.1), dimensions={0}, to_apply=%region_0.0 | reduce | flops 2031616 | bytes 8650756 | tf_op jit(solution)/shard_map/reduce_sum | solution.py:88
  100.2 3.3 collective-permute-done.2
  103.6 2.5 collective-permute-start.3
  109.4 2.5 collective-permute-start.4
  112.1 2.4 collective-permute-start.7
  123.1 3.9 collective-permute-start.8
  144.6 2.5 bitcast_multiply_fusion.3
  151.1 2.4 fusion.34
  158.0 3.1 broadcast_in_dim.38
  161.1 97.0 %dynamic_update_slice.10 = f32[2,512,1024]{2,0,1:T(2,128)} dynamic-update-slice(f32[2,512,1024]{2,0,1:T(2,128)} %broadcast_in_dim.38, f32[2,512,512]{2,0,1:T(2,128)S(1)} %copy.43, s32[]{:T(128)} %constant.119.clone.1, s32[]{:T(128)} %constant.119.clone.1, s32[]{:T(128)S(6)} %select_n.104) | dynamic-update-slice | bytes 4194308 | tf_op jit(solution)/shard_map/while/body/eval_jaxpr/transpose(jvp(jit(_roll_dynamic)))/dynamic_update_slice | solution.py:68
  264.5 3.9 pad_maximum_fusion.1
  270.4 71.9 %all-reduce.42.cloned.1.call-done = f32[3,512,512]{2,0,1:T(4,128)} async-done(((f32[3,512,512]{2,0,1:T(4,128)}), f32[3,512,512]{2,0,1:T(4,128)}) %all-reduce.42.cloned.1.call-update) | async-done | bytes 3145744
  343.3 2.4 collective-permute-start.10
  348.5 12.3 %gather_fusion.1 = f32[32,3,64,512]{3,1,2,0:T(4,128)} fusion(f32[3,96,512]{2,0,1:T(4,128)S(1)} %pad_maximum_fusion.2, s32[32]{0:T(128)S(1)} %get-tuple-element.112), kind=kCustom, calls=%fused_computation.1 | custom fusion | bytes 25166208 | tf_op jit(solution)/shard_map/vmap()/gather | solution.py:106
  360.7 15.5 %copy.44 = f32[32,3,64,512]{3,2,1,0:T(8,128)} copy(f32[32,3,64,512]{3,1,2,0:T(4,128)} %gather_fusion.1) | data formatting | bytes 25165824 | tf_op jit(solution)/shard_map/vmap()/gather | solution.py:106
  376.2 181.6 %all-reduce.40.cloned.1.call-done = f32[32,3,64,512]{3,2,1,0:T(8,128)} async-done(((f32[32,3,64,512]{3,2,1,0:T(8,128)}), f32[32,3,64,512]{3,2,1,0:T(8,128)}) %all-reduce.40.cloned.1.call-update) | async-done | bytes 12582928 | tf_op jit(solution)/shard_map/psum | solution.py:109
  557.9 2.9 fusion.1
  560.7 9.6 %fusion = f32[32,2,64,512]{3,2,1,0:T(8,128)} fusion(f32[32,2,64,512]{3,2,1,0:T(8,128)} %param.6, f32[32,3,64,512]{3,2,1,0:T(8,128)} %all-reduce.40.cloned.1.call-done, f32[32,64,512]{2,1,0:T(8,128)S(1)} %fusion.1), kind=kLoop, calls=%fused_computation.5 | loop fusion | flops 4194304 | bytes 29360128 | tf_op jit(solution)/shard_map/sub | solution.py:110
  (97 shorter events, 46.9 us)
Async XLA Ops:
  6.5 335.7 %all-reduce.42.cloned.1.call-start = ((), (), s32[]{:S(2)}) async-start(), calls=%async_computation.1 | async-start | bytes 8388608
  20.9 5.4 copy-start.5
  23.2 26.0 %collective-permute-start = (f32[32,2,16,512]{3,1,0,2:T(2,128)S(1)}, f32[32,2,16,512]{3,1,0,2:T(2,128)S(1)}, u32[]{:S(2)}, u32[]{:S(2)}) collective-permute-start(f32[32,2,16,512]{3,1,0,2:T(2,128)S(1)} %get-tuple-element.41), channel_id=1, source_target_pairs={{0,1},{1,2},{2,3},{3,4},{4,5},{5,6},{6,7},{7,0},{8,9},{9,10},{10,1... | collective-permute-start | bytes 6291464 | tf_op jit(solution)/shard_map/ppermute | solution.py:51
  26.2 25.5 %collective-permute-start.1 = (f32[32,2,16,512]{3,1,0,2:T(2,128)S(1)}, f32[32,2,16,512]{3,1,0,2:T(2,128)S(1)}, u32[]{:S(2)}, u32[]{:S(2)}) collective-permute-start(f32[32,2,16,512]{3,1,0,2:T(2,128)S(1)} %get-tuple-element.42), channel_id=1, source_target_pairs={{1,0},{2,1},{3,2},{4,3},{5,4},{6,5},{7,6},{0,7},{9,8},{10,9},{11,1... | collective-permute-start | bytes 6291464 | tf_op jit(solution)/shard_map/ppermute | solution.py:52
  94.0 23.6 %copy-start.4 = (s32[1,1,2]{2,1,0:T(1,128)S(1)}, s32[1,1,2]{2,1,0:T(1,128)}, u32[]{:S(2)}) copy-start(s32[1,1,2]{2,1,0:T(1,128)} %param.8) | copy-start | bytes 28
  100.2 3.3 collective-permute-start.2
  103.6 5.8 %collective-permute-start.3 = (f32[2,64,512]{2,1,0:T(8,128)S(1)}, f32[2,64,512]{2,1,0:T(8,128)S(1)}, u32[]{:S(2)}, u32[]{:S(2)}) collective-permute-start(f32[2,64,512]{2,1,0:T(8,128)S(1)} %collective-permute-done.2), channel_id=1, source_target_pairs={{0,1},{1,2},{2,3},{3,4},{4,5},{5,6},{6,7},{7,0},{8,9},{9,10},{10,1... | collective-permute-start | bytes 786440 | tf_op jit(solution)/shard_map/ppermute | solution.py:27
  106.0 6.1 %collective-permute-start.6 = (f32[2,64,512]{2,1,0:T(8,128)S(1)}, f32[2,64,512]{2,1,0:T(8,128)S(1)}, u32[]{:S(2)}, u32[]{:S(2)}) collective-permute-start(f32[2,64,512]{2,1,0:T(8,128)S(1)} %copy.39), channel_id=1, source_target_pairs={{1,0},{2,1},{3,2},{4,3},{5,4},{6,5},{7,6},{0,7},{9,8},{10,9},{11,1... | collective-permute-start | bytes 786440 | tf_op jit(solution)/shard_map/ppermute | solution.py:32
  109.4 6.2 %collective-permute-start.4 = (f32[2,64,512]{2,1,0:T(8,128)S(1)}, f32[2,64,512]{2,1,0:T(8,128)S(1)}, u32[]{:S(2)}, u32[]{:S(2)}) collective-permute-start(f32[2,64,512]{2,1,0:T(8,128)S(1)} %collective-permute-done.3), channel_id=1, source_target_pairs={{0,1},{1,2},{2,3},{3,4},{4,5},{5,6},{6,7},{7,0},{8,9},{9,10},{10,1... | collective-permute-start | bytes 786440 | tf_op jit(solution)/shard_map/ppermute | solution.py:27
  112.1 11.0 %collective-permute-start.7 = (f32[2,64,512]{2,1,0:T(8,128)S(1)}, f32[2,64,512]{2,1,0:T(8,128)S(1)}, u32[]{:S(2)}, u32[]{:S(2)}) collective-permute-start(f32[2,64,512]{2,1,0:T(8,128)S(1)} %collective-permute-done.6), channel_id=1, source_target_pairs={{1,0},{2,1},{3,2},{4,3},{5,4},{6,5},{7,6},{0,7},{9,8},{10,9},{11,1... | collective-permute-start | bytes 786440 | tf_op jit(solution)/shard_map/ppermute | solution.py:32
  115.5 11.5 %collective-permute-start.5 = (f32[2,64,512]{2,1,0:T(8,128)S(1)}, f32[2,64,512]{2,1,0:T(8,128)S(1)}, u32[]{:S(2)}, u32[]{:S(2)}) collective-permute-start(f32[2,64,512]{2,1,0:T(8,128)S(1)} %collective-permute-done.4), channel_id=1, source_target_pairs={{0,1},{1,2},{2,3},{3,4},{4,5},{5,6},{6,7},{7,0},{8,9},{9,10},{10,1... | collective-permute-start | bytes 786440 | tf_op jit(solution)/shard_map/ppermute | solution.py:27
  123.1 9.0 %collective-permute-start.8 = (f32[2,64,512]{2,1,0:T(8,128)S(1)}, f32[2,64,512]{2,1,0:T(8,128)S(1)}, u32[]{:S(2)}, u32[]{:S(2)}) collective-permute-start(f32[2,64,512]{2,1,0:T(8,128)S(1)} %collective-permute-done.7), channel_id=1, source_target_pairs={{1,0},{2,1},{3,2},{4,3},{5,4},{6,5},{7,6},{0,7},{9,8},{10,9},{11,1... | collective-permute-start | bytes 786440 | tf_op jit(solution)/shard_map/ppermute | solution.py:32
  136.0 1.6 copy-start.1
  138.4 1.2 copy-start
  143.6 1.0 copy-start.3
  258.2 2.2 copy-start.2
  268.4 0.7 copy-start.6
  268.5 289.4 %all-reduce.40.cloned.1.call-start = ((), (), s32[]{:S(2)}) async-start(), calls=%async_computation | async-start | bytes 25165824 | tf_op jit(solution)/shard_map/psum | solution.py:109
  343.3 4.4 collective-permute-start.10
  345.7 2.6 collective-permute-start.9
Sparse Core Ops, SparseCore 0:
  268.6 73.6 all-reduce.41
  376.4 181.4 all-reduce.39
